TPU v7x, 256 devices: a whole 4x4x8 slice. The times are simulated.
256 devices in a mesh: seq: 4 (over z_lo), row: 16 (over x, z_hi, core), col: 4 (over y).
Axes of the slice: x: 4, y: 4, z: 8 (z_hi: 2, z_lo: 4; z = z_hi * 4 + z_lo), core: 2. Of those that a mesh axis runs over, the one named last changes fastest.
Arguments:
- grads: bfloat16 [1024, 28672], P('row', ('seq', 'col')), may hold values from -6 to 6
- acts: bfloat16 [1024, 8192], P(('seq', 'col'), 'row'), may hold values from -6 to 6
- out_basis: bfloat16 [28672, 28672], P(('seq', 'col'), 'row'), may hold values from -0.03125 to 0.03125
- in_basis: bfloat16 [8192, 8192], P('row', ('seq', 'col')), may hold values from -0.0625 to 0.0625
- lengths: int32 [4], replicated, may hold values from 1 to 256, 768 in all
Outputs:
- eigenvalues: float32 [28672, 8192], P('row', ('seq', 'col'))
Inputs may be any that keep to these rules, and one draw needn't show every extreme that they name: lengths sum to 768; some sequence is full.
All inputs are finite; a program needn't handle non-finite values.
Results may differ from a plain program's by a relative error of at most 0.0036.
Values may be sent and summed in bfloat16 or wider, within the bound.
A program may use at most 64 MiB of HBM per device.

v0:
```python
import jax
import jax.numpy as jnp
from jax import lax
from jax.sharding import PartitionSpec as P

SEQ_LEN = 256


def copy_for_each(x, axis):
    copies = jnp.broadcast_to(x, (lax.axis_size(axis), *x.shape))
    return lax.all_to_all(copies, axis, split_axis=0, concat_axis=0, tiled=True)


def laid_out(tiles, dim):
    tiles = jnp.moveaxis(tiles, 0, dim)
    lengths = tiles.shape
    return tiles.reshape(*lengths[:dim], lengths[dim] * lengths[dim + 1], *lengths[dim + 2 :])


def gathered_copies(x, axis, dim):
    tiles = copy_for_each(x, axis)
    return laid_out(tiles, dim)


def in_blocks(x, dim, devices):
    before, after = (x.shape[:dim], x.shape[dim + 1 :])
    return jnp.moveaxis(x.reshape(*before, devices, -1, *after), dim, 0)


def sum_at_owner(x, axis, dim):
    tiles = in_blocks(x, dim, lax.axis_size(axis))
    arrived = lax.all_to_all(tiles, axis, split_axis=0, concat_axis=0, tiled=True)
    return arrived.sum(axis=0)


def body(grads, acts, out_basis, in_basis, lengths):
    seq_count = lax.axis_size("seq")
    partial_value = jnp.dot(
        lax.all_gather(grads, "row", axis=0, tiled=True),
        out_basis,
        preferred_element_type=jnp.float32,
    )
    grad_proj = lax.psum(partial_value, ("seq", "col")).astype(jnp.bfloat16)
    act_full = gathered_copies(acts, ("seq", "col"), 0)
    row_count = act_full.shape[0] // lax.axis_size("row")
    act_share = sum_at_owner(
        jnp.dot(act_full, in_basis, preferred_element_type=jnp.float32), "row", 0
    )
    token_index = lax.axis_index("row") * row_count + jnp.arange(row_count, dtype=jnp.int32)
    seq_owner = token_index // SEQ_LEN
    position = token_index % SEQ_LEN
    seq_ids = jnp.arange(lengths.shape[0], dtype=jnp.int32)
    seq_length = jnp.sum(
        jnp.where(seq_owner[:, None] == seq_ids[None, :], lengths[None, :], 0), axis=1
    )
    is_live = (position < seq_length).astype(jnp.float32)
    act_rows = (act_share * is_live[:, None]).astype(jnp.bfloat16)
    act_proj = lax.all_gather(act_rows, "row", axis=0, tiled=True)
    grad_three = grad_proj.reshape(seq_count, SEQ_LEN, grad_proj.shape[1])
    act_three = act_proj.reshape(seq_count, SEQ_LEN, act_proj.shape[1])

    def accumulate(total, pair):
        grad_seq = lax.dot_general(
            pair[0], pair[1], (((0,), (0,)), ((), ())), preferred_element_type=jnp.float32
        )
        return (total + grad_seq * grad_seq, None)

    start_total = jnp.zeros((grad_proj.shape[1], act_proj.shape[1]), jnp.float32)
    total, unused = lax.scan(accumulate, start_total, (grad_three, act_three))
    return total / (seq_count * SEQ_LEN)


def solution(mesh):
    in_specs = (
        P("row", ("seq", "col")),
        P(("seq", "col"), "row"),
        P(("seq", "col"), "row"),
        P("row", ("seq", "col")),
        P(),
    )
    out_specs = P("row", ("seq", "col"))
    return jax.shard_map(body, mesh=mesh, in_specs=in_specs, out_specs=out_specs, check_vma=False)
```

profile of v0, /device:TPU:1, one launch (start us, length us, event | category | flops | bytes accessed | tf_op | source)
XLA Modules:
  0.0 338.1 jit_solution(12403739180391516133)
XLA Ops:
  6.5 0.0 copy-start
  6.5 0.0 all-gather.3.cloned.1.call-start
  6.5 0.7 all-gather.3.cloned.1.call-update
  7.3 0.9 broadcast_in_dim.23
  8.2 38.8 %all_to_all.10 = bf16[16,64,512]{2,1,0:T(8,128)(2,1)S(1)} all-to-all(bf16[16,64,512]{2,1,0:T(8,128)(2,1)S(1)} %broadcast_in_dim.23), channel_id=1, replica_groups=mesh['seq'=4,'row'=16,'col'=4] {'seq','col'}, dimensions={0} | all-to-all | bytes 2097152 | tf_op jit(solution)/shard_map/all_to_all | solution.py:11
  47.0 0.0 copy-done
  47.0 0.0 copy-start.1
  47.0 2.0 fusion.5
  49.0 10.9 %all-to-all-start.1 = ((f32[16,64,512]{2,1,0:T(8,128)}), f32[16,64,512]{2,1,0:T(8,128)S(1)}, u32[]{:S(2)}, u32[]{:S(2)}) async-start(f32[16,64,512]{2,1,0:T(8,128)} %fusion.5), calls=%async_computation.1 | async-start | bytes 4194304 | tf_op jit(solution)/shard_map/all_to_all | solution.py:32
  60.0 0.0 all-gather.5.cloned.1.call-start
  60.0 0.0 copy-done.1
  60.0 0.1 select_reduce_fusion
  60.1 67.2 %all-to-all-done.1 = f32[16,64,512]{2,1,0:T(8,128)S(1)} async-done(((f32[16,64,512]{2,1,0:T(8,128)}), f32[16,64,512]{2,1,0:T(8,128)S(1)}, u32[]{:S(2)}, u32[]{:S(2)}) %all-to-all-start.1) | async-done | bytes 2097184 | tf_op jit(solution)/shard_map/all_to_all | solution.py:32
  127.3 0.2 reduce_sum.18
  127.5 0.7 multiply_convert_fusion
  128.2 0.0 all-gather.5.cloned.1.call-update
  128.2 0.0 all-gather.3.cloned.1.call-done
  128.3 12.2 %fusion.7 = f32[1024,1792]{1,0:T(8,128)} fusion(bf16[1024,1792]{1,0:T(8,128)(2,1)} %all-gather.3.cloned.1.call-done, bf16[1792,1792]{1,0:T(8,128)(2,1)} %param.9), kind=kOutput, calls=%fused_computation.20 | convolution fusion | flops 6576668672 | bytes 17432576 | tf_op jit(solution)/shard_map/dot_general | solution.py:38
  140.5 168.0 %all-reduce.1 = bf16[1024,1792]{1,0:T(8,128)(2,1)} all-reduce(f32[1024,1792]{1,0:T(8,128)} %fusion.7), channel_id=1, replica_groups=mesh['seq'=4,'row'=16,'col'=4] {'seq','col'}, use_global_device_ids=true, to_apply=%region_0.0 | all-reduce | flops 1835008 | bytes 11010048 | tf_op jit(solution)/shard_map/psum | solution.py:43
  308.5 0.0 all-gather.5.cloned.1.call-done
  308.5 18.5 %while.11 = (s32[]{:T(128)}, f32[1792,512]{1,0:T(8,128)}, bf16[4,256,1792]{2,1,0:T(8,128)(2,1)}, bf16[4,256,512]{2,1,0:T(8,128)(2,1)}, s32[]{:T(128)}, /*index=5*/s32[]{:T(128)}) while((s32[]{:T(128)}, f32[1792,512]{1,0:T(8,128)}, bf16[4,256,1792]{2,1,0:T(8,128)(2,1)}, bf16[4,256,512]{2,1,0:T(8,128)(2,1)}, s32[]{:T(128)}, ...), condition=%wide.region_4.5_spmd.clone, body=%wide.region_3.4_spmd.clone.sunk | while | flops 472514560 | bytes 8521302 | solution.py:69
  308.5 3.7 %select_add_fusion.2 = f32[1792,512]{1,0:T(8,128)} fusion(f32[1792,512]{1,0:T(8,128)} %get-tuple-element.83, pred[]{:T(512)S(6)} %compare.14, bf16[4,256,1792]{2,1,0:T(8,128)(2,1)} %get-tuple-element.90, s32[]{:T(128)S(6)} %copy.9, bf16[4,256,512]{2,1,0:T(8,128)(2,1)} %get-tuple-element.91), kind=kOutput, calls=%fused_computation.1.clone.1 | convolution fusion | flops 472514560 | bytes 8521216 | tf_op jit(solution)/shard_map/while/body/eval_jaxpr/dot_general | solution.py:63
  312.3 4.9 %select_add_fusion.2 = f32[1792,512]{1,0:T(8,128)} fusion(f32[1792,512]{1,0:T(8,128)} %get-tuple-element.83, pred[]{:T(512)S(6)} %compare.14, bf16[4,256,1792]{2,1,0:T(8,128)(2,1)} %get-tuple-element.90, s32[]{:T(128)S(6)} %copy.9, bf16[4,256,512]{2,1,0:T(8,128)(2,1)} %get-tuple-element.91), kind=kOutput, calls=%fused_computation.1.clone.1 | convolution fusion | flops 472514560 | bytes 8521216 | tf_op jit(solution)/shard_map/while/body/eval_jaxpr/dot_general | solution.py:63
  317.2 4.9 %select_add_fusion.2 = f32[1792,512]{1,0:T(8,128)} fusion(f32[1792,512]{1,0:T(8,128)} %get-tuple-element.83, pred[]{:T(512)S(6)} %compare.14, bf16[4,256,1792]{2,1,0:T(8,128)(2,1)} %get-tuple-element.90, s32[]{:T(128)S(6)} %copy.9, bf16[4,256,512]{2,1,0:T(8,128)(2,1)} %get-tuple-element.91), kind=kOutput, calls=%fused_computation.1.clone.1 | convolution fusion | flops 472514560 | bytes 8521216 | tf_op jit(solution)/shard_map/while/body/eval_jaxpr/dot_general | solution.py:63
  322.1 4.9 %select_add_fusion.2 = f32[1792,512]{1,0:T(8,128)} fusion(f32[1792,512]{1,0:T(8,128)} %get-tuple-element.83, pred[]{:T(512)S(6)} %compare.14, bf16[4,256,1792]{2,1,0:T(8,128)(2,1)} %get-tuple-element.90, s32[]{:T(128)S(6)} %copy.9, bf16[4,256,512]{2,1,0:T(8,128)(2,1)} %get-tuple-element.91), kind=kOutput, calls=%fused_computation.1.clone.1 | convolution fusion | flops 472514560 | bytes 8521216 | tf_op jit(solution)/shard_map/while/body/eval_jaxpr/dot_general | solution.py:63
  327.0 4.3 %broadcast_multiply_fusion = f32[1792,512]{1,0:T(8,128)} fusion(f32[1792,512]{1,0:T(8,128)} %get-tuple-element.27), kind=kLoop, calls=%fused_computation.7 | loop fusion | flops 917504 | bytes 7340032 | tf_op jit(solution)/shard_map/div | solution.py:70
  (3 shorter events, 0.0 us)
Async XLA Ops:
  6.5 40.4 %copy-start = (bf16[512,512]{1,0:T(8,128)(2,1)S(1)}, bf16[512,512]{1,0:T(8,128)(2,1)}, u32[]{:S(2)}) copy-start(bf16[512,512]{1,0:T(8,128)(2,1)} %param.10) | copy-start | bytes 1572868
  6.5 121.7 %all-gather.3.cloned.1.call-start = ((), (), s32[]{:S(2)}) async-start(), calls=%async_computation.2 | async-start | bytes 3899392 | tf_op jit(solution)/shard_map/all_gather | solution.py:39
  47.0 13.1 %copy-start.1 = (s32[4]{0:T(128)S(1)}, s32[4]{0:T(128)}, u32[]{:S(2)}) copy-start(s32[4]{0:T(128)} %param.11) | copy-start | bytes 52
  49.0 78.3 %all-to-all-start.1 = ((f32[16,64,512]{2,1,0:T(8,128)}), f32[16,64,512]{2,1,0:T(8,128)S(1)}, u32[]{:S(2)}, u32[]{:S(2)}) async-start(f32[16,64,512]{2,1,0:T(8,128)} %fusion.5), calls=%async_computation.1 | async-start | bytes 4194304 | tf_op jit(solution)/shard_map/all_to_all | solution.py:32
  60.0 248.6 %all-gather.5.cloned.1.call-start = ((), (), s32[]{:S(2)}) async-start(), calls=%async_computation.3 | async-start | bytes 1114112 | tf_op jit(solution)/shard_map/all_gather | solution.py:58
Sparse Core Ops, SparseCore 0:
  10.0 83.9 all-gather.2
  128.3 51.0 all-gather.4
where the time goes:
time: 341 us; the launch traced here: 338 us
  blocking collectives  207 us (61%)
  waiting for transfers between devices  67.9 us (20%)
  matrix products  32.7 us (10%)
  between operations  13.5 us (4%)
  starting transfers between devices  11 us (3%)
  other arithmetic  5.29 us (2%)
    psum x1, blocking collectives, body(): grad_proj = lax.psum(partial_value, ('seq', 'col')).astype(jnp.bfloat16)  168 us
    all_to_all x1, waiting for transfers between devices, sum_at_owner(): lax.all_to_all(tiles, axis, split_axis=0, concat_axis=0, tiled=True)  67.2 us
    all_to_all x1, blocking collectives, copy_for_each(): return lax.all_to_all(copies, axis, split_axis=0, concat_axis=0, tiled=True)  38.8 us
    dot_general x4, matrix products, accumulate(): lax.dot_general(pair[0], pair[1], (((0,), (0,)), ((), ())), preferred_ele...  18.5 us
    dot_general x1, matrix products, body(): jnp.dot(lax.all_gather(grads, 'row', axis=0, tiled=True), out_basis, pref...  12.2 us
    all_to_all x1, starting transfers between devices, sum_at_owner(): lax.all_to_all(tiles, axis, split_axis=0, concat_axis=0, tiled=True)  10.9 us
  transfers between devices with their start and end apart: 3, of which 1 were waited for; matrix products, arithmetic and copies ran while one was open for 5% of the time, Pallas kernels for 0%

commit v1 on v0

v1 whole, which is shorter than its diff:
```python
import functools

import jax
import jax.numpy as jnp
from jax import lax
from jax.experimental import pallas as pl
from jax.experimental.pallas import tpu as pltpu
from jax.sharding import PartitionSpec as P

SEQ = 256
LIVE = 768
PIECE = 48
COLS = 256
MESH = pl.DeviceIdType.MESH
F32, BF16 = jnp.float32, jnp.bfloat16


def kernel(
    chunks,
    len_ref, grads_ref, acts_ref, ob_ref, ib_ref, out_ref,
    xg, xa, ob, ib, gc, ac,
    pf, y1s, y1r, y2s, y2r, zs, zr, gp,
    pa, kr, x1r, x2r, hr, ap, am, gt, ob_out,
    loc, out_sem, g_s, g_r, a_s, a_r, p_s, p_r, c_s, c_r,
):
    s, r, c = lax.axis_index("seq"), lax.axis_index("row"), lax.axis_index("col")
    core, half, x = r % 2, (r // 2) % 2, r // 4
    xp, xm, x2 = (x + 1) % 4, (x + 3) % 4, (x + 2) % 4
    cp, cm, c2 = (c + 1) % 4, (c + 3) % 4, (c + 2) % 4

    def row_of(x_at, half_at, core_at):
        return x_at * 4 + half_at * 2 + core_at

    to_core = {"row": row_of(x, half, 1 - core)}
    to_half = {"row": row_of(x, 1 - half, core)}
    to_xp, to_xm = {"row": row_of(xp, half, core)}, {"row": row_of(xm, half, core)}
    to_cp, to_cm = {"col": cp}, {"col": cm}
    to_seq = [{"seq": (s + d) % 4} for d in (1, 2, 3)]

    def remote(src, dst, send, recv, to):
        return pltpu.make_async_remote_copy(
            src_ref=src, dst_ref=dst, send_sem=send, recv_sem=recv, device_id=to, device_id_type=MESH
        )

    load_g = pltpu.make_async_copy(grads_ref, xg.at[r], loc.at[0])
    load_a = pltpu.make_async_copy(acts_ref, xa.at[c, s], loc.at[1])
    load_ib = pltpu.make_async_copy(ib_ref, ib, loc.at[2])
    load_ob = pltpu.make_async_copy(ob_ref, ob, loc.at[3])
    load_g.start()
    load_a.start()

    barrier = pltpu.get_barrier_semaphore()
    for to in (to_core, to_half, to_xp, to_xm, to_cp, to_cm, *to_seq):
        pl.semaphore_signal(barrier, inc=1, device_id=to, device_id_type=MESH)
    load_g.wait()
    load_a.wait()
    pl.semaphore_wait(barrier, 9)

    def block(x_at, half_at, core_at):
        return xg.at[row_of(x_at, half_at, core_at)]

    mine, other = block(x, half, core), block(x, 1 - half, core)
    n_send = [0]
    sends = []

    def send_g(src, recv, to):
        cp_ = remote(src, src, g_s.at[n_send[0]], g_r.at[recv], to)
        n_send[0] += 1
        cp_.start()
        sends.append(cp_)

    def got_g(dst, recv):
        remote(dst, dst, g_s.at[0], g_r.at[recv], to_core).wait_recv()

    send_g(mine.at[0], 2, to_xp)
    send_g(mine.at[1], 5, to_xm)
    send_g(mine.at[0], 0, to_half)
    send_g(mine.at[1], 1, to_half)
    send_g(mine.at[1], 3, to_xp)
    send_g(mine.at[0], 4, to_xm)
    send_g(mine, 14, to_core)

    a_sends = []

    def send_a(src, i, to):
        cp_ = remote(src, src, a_s.at[i], a_r.at[i], to)
        cp_.start()
        a_sends.append(cp_)

    def got_a(dst, i):
        remote(dst, dst, a_s.at[i], a_r.at[i], to_core).wait_recv()

    for d in range(3):
        send_a(xa.at[c, s], d, to_seq[d])
    load_ib.start()
    load_ob.start()

    got_g(block(xm, half, core).at[0], 2)
    send_g(block(xm, half, core).at[0], 6, to_xp)
    got_g(block(xp, half, core).at[1], 5)
    send_g(block(xp, half, core).at[1], 7, to_xm)

    for d in range(3):
        got_a(xa.at[c, (s + 3 - d) % 4], d)
    send_a(xa.at[c], 3, to_cp)
    send_a(xa.at[c], 4, to_cm)

    got_g(other.at[0], 0)
    send_g(other.at[0], 8, to_xp)
    send_g(other.at[0], 10, to_xm)
    got_g(block(xm, half, core).at[1], 3)
    send_g(block(xm, half, core), 15, to_core)
    got_g(block(xp, half, core).at[0], 4)
    send_g(block(xp, half, core), 16, to_core)
    got_g(other.at[1], 1)
    send_g(other.at[1], 11, to_xm)
    send_g(other.at[1], 9, to_xp)
    send_g(other, 17, to_core)
    got_g(block(x2, half, core).at[0], 6)
    got_g(block(x2, half, core).at[1], 7)
    send_g(block(x2, half, core), 18, to_core)

    got_a(xa.at[cm], 3)
    send_a(xa.at[cm, 0:2], 5, to_cp)
    got_a(xa.at[cp], 4)
    send_a(xa.at[cp, 2:4], 6, to_cm)

    got_g(block(xm, 1 - half, core).at[0], 8)
    send_g(block(xm, 1 - half, core).at[0], 12, to_xp)
    got_g(block(xp, 1 - half, core).at[1], 11)
    send_g(block(xp, 1 - half, core).at[1], 13, to_xm)

    lens = [len_ref[q] for q in range(4)]
    offs = [jnp.int32(0)]
    for q in range(3):
        offs.append(offs[-1] + lens[q])

    def pick(i):
        rows = lax.broadcasted_iota(jnp.int32, (SEQ, SEQ), 0) + i * SEQ
        slot = lax.broadcasted_iota(jnp.int32, (SEQ, SEQ), 1)
        tiles = []
        for q in (i, i + 1):
            hit = jnp.logical_and(rows == slot + offs[q], slot < lens[q])
            tiles.append(jnp.where(hit, 1.0, 0.0).astype(BF16))
        return jnp.concatenate(tiles, axis=1)

    got_a(xa.at[c2, 0:2], 5)
    got_a(xa.at[c2, 2:4], 6)
    load_ib.wait()
    for i in range(3):
        rows = jnp.concatenate([xa[b, q] for q in (i, i + 1) for b in range(4)], axis=0)
        packed = jnp.dot(pick(i), rows, preferred_element_type=F32)
        ac[i * SEQ : (i + 1) * SEQ, :] = packed.astype(BF16)
    pa[...] = jnp.dot(ac[...], ib[...], preferred_element_type=F32).reshape(pa.shape)

    p_sends = []

    def send_p(src, dst, i, to):
        cp_ = remote(src, dst, p_s.at[i], p_r.at[i], to)
        cp_.start()
        return cp_

    def got_p(dst, i):
        remote(dst, dst, p_s.at[i], p_r.at[i], to_core).wait_recv()

    send_p(pa.at[1 - core], kr, 0, to_core)

    got_g(block(xm, 1 - half, core).at[1], 9)
    send_g(block(xm, 1 - half, core), 19, to_core)
    got_g(block(xp, 1 - half, core).at[0], 10)
    send_g(block(xp, 1 - half, core), 20, to_core)
    got_g(block(x2, 1 - half, core).at[0], 12)
    got_g(block(x2, 1 - half, core).at[1], 13)
    send_g(block(x2, 1 - half, core), 21, to_core)
    for n, (x_at, half_at) in enumerate(
        ((x, half), (xm, half), (xp, half), (x, 1 - half), (x2, half), (xm, 1 - half), (xp, 1 - half), (x2, 1 - half))
    ):
        got_g(block(x_at, half_at, 1 - core), 14 + n)

    for i in range(3):
        chosen = pick(i)

        def packed_columns(j, carry, i=i, chosen=chosen):
            cols = pl.ds(pl.multiple_of(j * COLS, COLS), COLS)
            rows = xg[4 * i : 4 * i + 8, :, :, cols].reshape(2 * SEQ, COLS)
            packed = jnp.dot(chosen, rows, preferred_element_type=F32)
            gc[i * SEQ : (i + 1) * SEQ, cols] = packed.astype(BF16)
            return carry

        lax.fori_loop(0, chunks, packed_columns, 0)
    load_ob.wait()

    def c_copy(src, dst, i, n, to):
        return remote(src, dst, c_s.at[i, n], c_r.at[i, n], to)

    def multiply(i):
        cols = pl.ds(pl.multiple_of(i * COLS, COLS), COLS)
        pf[i] = jnp.dot(gc[...], ob[:, cols], preferred_element_type=F32).reshape(pf.shape[1:])
        y1s[i] = pf[i, c2].astype(BF16)

    def y1_copies(i):
        return (
            c_copy(y1s.at[i, 0:2], y1r.at[i, 0], i, 0, to_cp),
            c_copy(y1s.at[i, 2:4], y1r.at[i, 1], i, 1, to_cm),
        )

    def y2_copies(i):
        return (
            c_copy(y2s.at[i, 0], y2r.at[i, 0], i, 2, to_cp),
            c_copy(y2s.at[i, 1], y2r.at[i, 1], i, 3, to_cm),
        )

    def z_copies(i):
        return tuple(
            c_copy(zs.at[i, (s + d) % 4], zr.at[i, d - 1], i, 3 + d, to_seq[d - 1]) for d in (1, 2, 3)
        )

    def za_copies(i):
        return tuple(c_copy(gp.at[i, c, s], gp.at[i, c, s], i, 6 + d, to_seq[d - 1]) for d in (1, 2, 3))

    def ya1_copies(i):
        return (
            c_copy(gp.at[i, c], gp.at[i, c], i, 10, to_cp),
            c_copy(gp.at[i, c], gp.at[i, c], i, 11, to_cm),
        )

    def ya2_copies(i):
        return (
            c_copy(gp.at[i, cm, 0:2], gp.at[i, cm, 0:2], i, 12, to_cp),
            c_copy(gp.at[i, cp, 2:4], gp.at[i, cp, 2:4], i, 13, to_cm),
        )

    def start(copies):
        for copy in copies:
            copy.start()

    def arrived(copies):
        for copy in copies:
            copy.wait_recv()

    def out_copy(i):
        rows = pl.ds(pl.multiple_of(i * COLS, COLS), COLS)
        return pltpu.make_async_copy(ob_out.at[i], out_ref.at[rows], out_sem.at[i])

    def step(t, carry):
        @pl.when(t < chunks)
        def _():
            multiply(t)
            start(y1_copies(t))

        @pl.when(jnp.logical_and(t >= 1, t < chunks + 1))
        def _():
            i = t - 1
            arrived(y1_copies(i))
            y2s[i, 0, 0:2] = (pf[i, cp, 0:2] + y1r[i, 0].astype(F32)).astype(BF16)
            y2s[i, 0, 2:4] = pf[i, cp, 2:4].astype(BF16)
            y2s[i, 1, 0:2] = pf[i, cm, 0:2].astype(BF16)
            y2s[i, 1, 2:4] = (pf[i, cm, 2:4] + y1r[i, 1].astype(F32)).astype(BF16)
            start(y2_copies(i))

        @pl.when(jnp.logical_and(t >= 2, t < chunks + 2))
        def _():
            i = t - 2
            arrived(y2_copies(i))
            total = pf[i, c] + y2r[i, 0].astype(F32) + y2r[i, 1].astype(F32)
            pf[i, c] = total
            zs[i] = total.astype(BF16)
            start(z_copies(i))

        @pl.when(jnp.logical_and(t >= 3, t < chunks + 3))
        def _():
            i = t - 3
            arrived(z_copies(i))
            total = pf[i, c, s]
            for d in range(3):
                total = total + zr[i, d].astype(F32)
            gp[i, c, s] = total.astype(BF16)
            start(za_copies(i))

        @pl.when(jnp.logical_and(t >= 4, t < chunks + 4))
        def _():
            i = t - 4
            for d in range(3):
                piece = gp.at[i, c, (s + 3 - d) % 4]
                c_copy(piece, piece, i, 7 + d, to_core).wait_recv()
            start(ya1_copies(i))

        @pl.when(jnp.logical_and(t >= 5, t < chunks + 5))
        def _():
            i = t - 5
            c_copy(gp.at[i, cm], gp.at[i, cm], i, 10, to_core).wait_recv()
            c_copy(gp.at[i, cp], gp.at[i, cp], i, 11, to_core).wait_recv()
            start(ya2_copies(i))

        @pl.when(t == 0)
        def _():
            got_p(kr, 0)
            pa[core] = pa[core] + kr[...]
            send_p(pa.at[core, x2, 0], x1r.at[0], 1, to_xp)
            send_p(pa.at[core, x2, 1], x1r.at[1], 2, to_xm)

        @pl.when(t == 1)
        def _():
            got_p(x1r.at[0], 1)
            got_p(x1r.at[1], 2)
            pa[core, xp, 0] = pa[core, xp, 0] + x1r[0]
            pa[core, xm, 1] = pa[core, xm, 1] + x1r[1]
            send_p(pa.at[core, xp], x2r.at[0], 3, to_xp)
            send_p(pa.at[core, xm], x2r.at[1], 4, to_xm)

        @pl.when(t == 2)
        def _():
            got_p(x2r.at[0], 3)
            got_p(x2r.at[1], 4)
            pa[core, x] = pa[core, x] + x2r[0] + x2r[1]
            send_p(pa.at[core, x, 1 - half], hr, 5, to_half)

        @pl.when(t == 3)
        def _():
            got_p(hr, 5)
            ap[core, x, half] = (pa[core, x, half] + hr[...]).astype(BF16)
            send_p(ap.at[core, x, half], ap.at[core, x, half], 6, to_half)

        @pl.when(t == 4)
        def _():
            got_p(ap.at[core, x, 1 - half], 6)
            send_p(ap.at[core, x], ap.at[core, x], 7, to_xp)
            send_p(ap.at[core, x], ap.at[core, x], 8, to_xm)

        @pl.when(t == 5)
        def _():
            got_p(ap.at[core, xm], 7)
            got_p(ap.at[core, xp], 8)
            send_p(ap.at[core, xm, 0], ap.at[core, xm, 0], 9, to_xp)
            send_p(ap.at[core, xp, 1], ap.at[core, xp, 1], 10, to_xm)

        @pl.when(t == 6)
        def _():
            got_p(ap.at[core, x2, 0], 9)
            got_p(ap.at[core, x2, 1], 10)
            send_p(ap.at[core], ap.at[core], 11, to_core)

        @pl.when(t == 7)
        def _():
            got_p(ap.at[1 - core], 11)
            place = 0
            for q, (low, high) in enumerate(((0, 1), (0, 2), (1, 3), (2, 3))):
                for b in range(low, high):
                    rows = lax.broadcasted_iota(jnp.int32, (SEQ, ap.shape[-1]), 0) + b * SEQ
                    inside = jnp.logical_and(rows >= offs[q], rows < offs[q] + lens[q])
                    share = ap[...].reshape(LIVE, ap.shape[-1])[b * SEQ : (b + 1) * SEQ]
                    am[place : place + SEQ, :] = jnp.where(inside, share.astype(F32), 0.0).astype(BF16)
                    place += SEQ

        @pl.when(t >= 7)
        def _():
            i = t - 7
            c_copy(gp.at[i, c2, 0:2], gp.at[i, c2, 0:2], i, 12, to_core).wait_recv()
            c_copy(gp.at[i, c2, 2:4], gp.at[i, c2, 2:4], i, 13, to_core).wait_recv()
            gt[...] = gp[i].reshape(LIVE, COLS).T
            total, place = None, 0
            for low, high in ((0, 1), (0, 2), (1, 3), (2, 3)):
                depth = (high - low) * SEQ
                one = jnp.dot(
                    gt[:, low * SEQ : high * SEQ], am[place : place + depth, :], preferred_element_type=F32
                )
                total = one * one if total is None else total + one * one
                place += depth
            ob_out[i] = total * (1.0 / (4 * SEQ))
            out_copy(i).start()

        return carry

    lax.fori_loop(0, chunks + 7, step, 0)

    for copy in sends:
        copy.wait_send()
    for copy in a_sends:
        copy.wait_send()
    remote(pa.at[1 - core], kr, p_s.at[0], p_r.at[0], to_core).wait_send()
    for i in (1, 2):
        remote(x1r.at[0], x1r.at[0], p_s.at[i], p_r.at[i], to_core).wait_send()
    for i in (3, 4):
        remote(x2r.at[0], x2r.at[0], p_s.at[i], p_r.at[i], to_core).wait_send()
    remote(hr, hr, p_s.at[5], p_r.at[5], to_core).wait_send()
    remote(ap.at[core, x, half], ap.at[core, x, half], p_s.at[6], p_r.at[6], to_half).wait_send()
    for i in (7, 8):
        remote(ap.at[core, x], ap.at[core, x], p_s.at[i], p_r.at[i], to_xp).wait_send()
    for i in (9, 10):
        remote(ap.at[core, x, 0], ap.at[core, x, 0], p_s.at[i], p_r.at[i], to_xp).wait_send()
    remote(ap.at[core], ap.at[core], p_s.at[11], p_r.at[11], to_core).wait_send()

    def finish(i, carry):
        for copies in (y1_copies, y2_copies, z_copies, za_copies, ya1_copies, ya2_copies):
            for copy in copies(i):
                copy.wait_send()
        out_copy(i).wait()
        return carry

    lax.fori_loop(0, chunks, finish, 0)


def body(grads, acts, out_basis, in_basis, lengths):
    n_row, n_seq, n_col = lax.axis_size("row"), lax.axis_size("seq"), lax.axis_size("col")
    tokens, width = grads.shape
    a_width = acts.shape[1]
    directions, a_directions = out_basis.shape[1], in_basis.shape[1]
    chunks = directions // COLS
    piece = (PIECE, COLS)
    dma = pltpu.SemaphoreType.DMA
    return pl.pallas_call(
        functools.partial(kernel, chunks),
        out_shape=jax.ShapeDtypeStruct((directions, a_directions), F32),
        in_specs=[pl.BlockSpec(memory_space=pltpu.SMEM)] + [pl.BlockSpec(memory_space=pl.ANY)] * 4,
        out_specs=pl.BlockSpec(memory_space=pl.ANY),
        scratch_shapes=[
            pltpu.VMEM((n_row, 2, tokens // 2, width), BF16),
            pltpu.VMEM((n_col, n_seq, tokens, a_width), BF16),
            pltpu.VMEM(out_basis.shape, BF16),
            pltpu.VMEM(in_basis.shape, BF16),
            pltpu.VMEM((LIVE, width), BF16),
            pltpu.VMEM((LIVE, a_width), BF16),
            pltpu.VMEM((chunks, 4, 4, *piece), F32),
            pltpu.VMEM((chunks, 4, *piece), BF16),
            pltpu.VMEM((chunks, 2, 2, *piece), BF16),
            pltpu.VMEM((chunks, 2, 4, *piece), BF16),
            pltpu.VMEM((chunks, 2, 4, *piece), BF16),
            pltpu.VMEM((chunks, 4, *piece), BF16),
            pltpu.VMEM((chunks, 3, *piece), BF16),
            pltpu.VMEM((chunks, 4, 4, *piece), BF16),
            pltpu.VMEM((2, 4, 2, PIECE, a_directions), F32),
            pltpu.VMEM((4, 2, PIECE, a_directions), F32),
            pltpu.VMEM((2, PIECE, a_directions), F32),
            pltpu.VMEM((2, 2, PIECE, a_directions), F32),
            pltpu.VMEM((PIECE, a_directions), F32),
            pltpu.VMEM((2, 4, 2, PIECE, a_directions), BF16),
            pltpu.VMEM((6 * SEQ, a_directions), BF16),
            pltpu.VMEM((COLS, LIVE), BF16),
            pltpu.VMEM((chunks, COLS, a_directions), F32),
            dma((4,)),
            dma((chunks,)),
            dma((22,)),
            dma((22,)),
            dma((7,)),
            dma((7,)),
            dma((12,)),
            dma((12,)),
            dma((chunks, 14)),
            dma((chunks, 14)),
        ],
        compiler_params=pltpu.CompilerParams(
            collective_id=0, has_side_effects=True, vmem_limit_bytes=60 * 1024 * 1024
        ),
        name="eigen",
    )(lengths, grads.reshape(2, tokens // 2, width), acts, out_basis, in_basis)


def solution(mesh):
    in_specs = (
        P("row", ("seq", "col")),
        P(("seq", "col"), "row"),
        P(("seq", "col"), "row"),
        P("row", ("seq", "col")),
        P(),
    )
    out_specs = P("row", ("seq", "col"))
    return jax.shard_map(body, mesh=mesh, in_specs=in_specs, out_specs=out_specs, check_vma=False)
```

time: 341 us -> 117 us (0.34)
  blocking collectives: 207 us -> 0 us
  Pallas kernels: 0 us -> 110 us
  waiting for transfers between devices: 67.9 us -> 0 us
  matrix products: 32.7 us -> 0 us
  between operations: 13.5 us -> 0.01 us
  starting transfers between devices: 11 us -> 0 us
  other arithmetic: 5.29 us -> 0 us
    psum x1 -> x0, blocking collectives: 168 us -> none  [body(): grad_proj = lax.psum(partial_value, ('seq', 'col')).astype(jnp.bfloat16)]
    pallas_call x0 -> x1, Pallas kernels: none -> 110 us  [body(): pl.pallas_call(functools.partial(kernel, chunks), out_shape=jax.ShapeDtyp...]
    all_to_all x1 -> x0, waiting for transfers between devices: 67.2 us -> none  [sum_at_owner(): lax.all_to_all(tiles, axis, split_axis=0, concat_axis=0, tiled=True)]
    all_to_all x1 -> x0, blocking collectives: 38.8 us -> none  [copy_for_each(): return lax.all_to_all(copies, axis, split_axis=0, concat_axis=0, tiled=True)]
    dot_general x6 -> x0, matrix products: 32.7 us -> none  [the longest x4 18.5 us: accumulate(): lax.dot_general(pair[0], pair[1], (((0,), (0,)), ((), ())), preferred_ele...]
    all_to_all x1 -> x0, starting transfers between devices: 10.9 us -> none  [sum_at_owner(): lax.all_to_all(tiles, axis, split_axis=0, concat_axis=0, tiled=True)]
    div x1 -> x0, other arithmetic: 4.31 us -> none  [body(): return total / (seq_count * SEQ_LEN)]
    unnamed x4 -> x1, local copies, waits for them, and re-layouts: 0.01 us -> 4.25 us
  transfers between devices with their start and end apart: 3 -> 0, of which waited for: 1 -> 0; matrix products, arithmetic and copies ran while one was open for 5% -> 0% of each run, Pallas kernels for 0% -> 0%
where the time goes in v1:
time: 117 us; the launch traced here: 115 us
  Pallas kernels  110 us (94%)
  local copies, waits for them, and re-layouts  4.25 us (4%)
    pallas_call x1, Pallas kernels, body(): pl.pallas_call(functools.partial(kernel, chunks), out_shape=jax.ShapeDtyp...  110 us
    unnamed x1, local copies, waits for them, and re-layouts  4.25 us

profile of v1, /device:TPU:1, one launch (start us, length us, event | category | flops | bytes accessed | tf_op | source)
XLA Modules:
  0.0 114.7 jit_solution(5769272563606492994)
XLA Ops:
  0.0 110.4 %eigen.1 = f32[1792,512]{1,0:T(8,128)} custom-call(s32[4]{0:T(128)} %len_ref.1, bf16[2,32,1792]{2,1,0:T(8,128)(2,1)} %bitcast.1, bf16[64,512]{1,0:T(8,128)(2,1)} %acts_ref.1, bf16[1792,1792]{1,0:T(8,128)(2,1)} %ob_ref.1, bf16[512,512]{1,0:T(8,128)(2,1)} %ib_ref.1), custom_call_target="tpu_custom_call" | custom-call | tf_op jit(solution)/shard_map/eigen/pallas_call | solution.py:411
  110.4 4.2 %copy.7 = f32[1792,512]{1,0:T(8,128)} copy(f32[1792,512]{1,0:T(8,128)} %eigen.1) | data formatting | bytes 7340032

commit v2 on v0

v2 whole, which is shorter than its diff:
```python
import functools

import jax
import jax.numpy as jnp
from jax import lax
from jax.experimental import pallas as pl
from jax.experimental.pallas import tpu as pltpu
from jax.sharding import PartitionSpec as P

SEQ = 256
HALF = 128
LIVE = 768
PIECE = 48
COLS = 256
MESH = pl.DeviceIdType.MESH
F32, BF16 = jnp.float32, jnp.bfloat16


def kernel(
    chunks,
    len_ref, grads_ref, acts_ref, ob_ref, ib_ref, out_ref,
    xg, xa, ob, ib, gc, ac,
    pf0, y1s0, y1r0, y2s0, y2r0, zs0, zr0, gp0,
    pf1, y1s1, y1r1, y2s1, y2r1, zs1, zr1, gp1,
    pa, kr, x1r, x2r, hr, ap, am, gt, res,
    loc, out_sem, g_s, g_r, a_s, a_r, p_s, p_r, c_s0, c_r0, c_s1, c_r1,
):
    s, r, c = lax.axis_index("seq"), lax.axis_index("row"), lax.axis_index("col")
    core, half, x = r % 2, (r // 2) % 2, r // 4
    xp, xm, x2 = (x + 1) % 4, (x + 3) % 4, (x + 2) % 4
    cp, cm, c2 = (c + 1) % 4, (c + 3) % 4, (c + 2) % 4

    def row_of(x_at, half_at, core_at):
        return x_at * 4 + half_at * 2 + core_at

    to_core = {"row": row_of(x, half, 1 - core)}
    to_half = {"row": row_of(x, 1 - half, core)}
    to_xp, to_xm = {"row": row_of(xp, half, core)}, {"row": row_of(xm, half, core)}
    to_cp, to_cm = {"col": cp}, {"col": cm}
    to_seq = [{"seq": (s + d) % 4} for d in (1, 2, 3)]

    def remote(src, dst, send, recv, to):
        return pltpu.make_async_remote_copy(
            src_ref=src, dst_ref=dst, send_sem=send, recv_sem=recv, device_id=to, device_id_type=MESH
        )

    load_g = pltpu.make_async_copy(grads_ref, xg.at[x, half, core], loc.at[0])
    load_a = pltpu.make_async_copy(acts_ref, xa.at[c, s], loc.at[1])
    load_ib = pltpu.make_async_copy(ib_ref, ib, loc.at[2])
    load_ob = pltpu.make_async_copy(ob_ref, ob, loc.at[3])
    load_g.start()
    load_a.start()

    barrier = pltpu.get_barrier_semaphore()
    for to in (to_core, to_half, to_xp, to_xm, to_cp, to_cm, *to_seq):
        pl.semaphore_signal(barrier, inc=1, device_id=to, device_id_type=MESH)
    load_g.wait()
    load_a.wait()
    pl.semaphore_wait(barrier, 9)

    def block(x_at, half_at, core_at):
        return xg.at[x_at, half_at, core_at]

    mine, other = block(x, half, core), block(x, 1 - half, core)
    def send_g(src, recv, to, group=1):
        remote(src, src, g_s.at[group], g_r.at[recv], to).start()

    def to_partner(src, base):
        remote(src, src, g_s.at[2], g_r.at[14 + base], to_core).start()

    def got_g(dst, recv):
        remote(dst, dst, g_s.at[0], g_r.at[recv], to_core).wait_recv()

    def near(base):
        return block(xm, 1 - half if base else half, core)

    def far(base):
        return block(xp, 1 - half if base else half, core)

    def relay_low(base):
        got_g(near(base).at[0], 2 + 6 * base)
        send_g(near(base).at[0], 6 + 6 * base, to_xp)

    def relay_high(base):
        got_g(far(base).at[1], 5 + 6 * base)
        send_g(far(base).at[1], 6 + 6 * base, to_xm)

    def near_to_core(base):
        got_g(near(base).at[1], 3 + 6 * base)
        to_partner(near(base), base)

    def far_to_core(base):
        got_g(far(base).at[0], 4 + 6 * base)
        to_partner(far(base), base)

    def other_low():
        got_g(other.at[0], 0)
        send_g(other.at[0], 8, to_xp)
        send_g(other.at[0], 10, to_xm)

    def other_high():
        got_g(other.at[1], 1)
        send_g(other.at[1], 11, to_xm)
        send_g(other.at[1], 9, to_xp)
        to_partner(other, 1)

    def third(base):
        opposite = block(x2, 1 - half if base else half, core)
        got_g(opposite, 6 + 6 * base)
        to_partner(opposite, base)

    def from_core(base):
        got_g(gc.at[0:SEQ], 14 + base)

    def send_a(src, i, to):
        remote(src, src, a_s.at[i], a_r.at[i], to).start()

    def got_a(dst, i):
        remote(dst, dst, a_s.at[i], a_r.at[i], to_core).wait_recv()

    def acts_seq():
        for d in range(3):
            send_a(xa.at[c, s], 0, to_seq[d])

    def begin():
        send_g(mine.at[0], 2, to_xp, 0)
        send_g(mine.at[1], 5, to_xm, 0)
        send_g(mine.at[0], 0, to_half)

    def begin_rest():
        remote(mine, mine, g_s.at[0], g_r.at[0], to_core).wait_send()
        send_g(mine.at[1], 3, to_xp)
        send_g(mine.at[0], 4, to_xm)
        send_g(mine.at[1], 1, to_half)
        to_partner(mine, 0)

    def acts_col():
        got_a(xa.at[c, 0:3], 0)
        send_a(xa.at[c], 1, to_cp)
        send_a(xa.at[c], 1, to_cm)

    def acts_pass():
        got_a(xa.at[0:2], 1)
        send_a(xa.at[cm, 0:2], 2, to_cp)
        send_a(xa.at[cp, 2:4], 2, to_cm)

    lens = [len_ref[q] for q in range(4)]
    first = [jnp.minimum(n, HALF) for n in lens]
    last = [jnp.maximum(n - HALF, 0) for n in lens]

    def runs(start, counts):
        places = []
        for n in counts:
            places.append((start, n))
            start = start + n
        return places, start

    natural_first, n_first = runs(0, first)
    natural_last, _ = runs(n_first, last)
    own, n_own = runs(0, [jnp.where(half == 0, f, l) for f, l in zip(first, last)])
    rest, _ = runs(n_own, [jnp.where(half == 0, l, f) for f, l in zip(first, last)])

    def pick(places, base):
        rows = lax.broadcasted_iota(jnp.int32, (SEQ, HALF), 0) + base
        slot = lax.broadcasted_iota(jnp.int32, (SEQ, HALF), 1)
        tiles = []
        for start_, n in places:
            hit = jnp.logical_and(rows == slot + start_, slot < n)
            tiles.append(jnp.where(hit, 1.0, 0.0).astype(BF16))
        return jnp.concatenate(tiles, axis=1)

    def pack(b):
        parts = []
        if b < 2:
            parts.append((half, pick(own, b * SEQ)))
        if b > 0:
            parts.append((1 - half, pick(rest, b * SEQ)))

        def columns(j, carry):
            cols = pl.ds(pl.multiple_of(j * COLS, COLS), COLS)
            packed = None
            for half_at, chosen in parts:
                rows = xg[:, half_at, :, :, :, cols].reshape(2 * SEQ, COLS)
                one = jnp.dot(chosen, rows, preferred_element_type=F32)
                packed = one if packed is None else packed + one
            gc[b * SEQ : (b + 1) * SEQ, cols] = packed.astype(BF16)
            return carry

        lax.fori_loop(0, chunks, columns, 0)

    def project_inputs():
        got_a(xa.at[0], 2)
        load_ib.wait()
        low = jnp.concatenate([xa[b, q] for q in range(4) for b in (0, 1)], axis=0)
        high = jnp.concatenate([xa[b, q] for q in range(4) for b in (2, 3)], axis=0)
        for b in range(3):
            packed = None
            for use, places, rows in ((b < 2, natural_first, low), (b > 0, natural_last, high)):
                if use:
                    one = jnp.dot(pick(places, b * SEQ), rows, preferred_element_type=F32)
                    packed = one if packed is None else packed + one
            ac[b * SEQ : (b + 1) * SEQ, :] = packed.astype(BF16)
        pa[...] = jnp.dot(ac[...], ib[...], preferred_element_type=F32).reshape(pa.shape)
        send_p(pa.at[1 - core], kr, 0, to_core)

    def send_p(src, dst, i, to):
        remote(src, dst, p_s.at[i], p_r.at[i], to).start()

    def got_p(dst, i):
        remote(dst, dst, p_s.at[i], p_r.at[i], to_core).wait_recv()

    def part(low, high, pf, y1s, y1r, y2s, y2r, zs, zr, gp, c_s, c_r):
        def send(src, dst, i, n, to):
            remote(src, dst, c_s.at[n], c_r.at[i, n], to).start()

        def got(dst, i, n):
            remote(dst, dst, c_s.at[n], c_r.at[i, n], to_core).wait_recv()

        def multiply(i):
            cols = pl.ds(i * COLS if isinstance(i, int) else pl.multiple_of(i * COLS, COLS), COLS)
            pf[i] = jnp.dot(gc[low:high, :], ob[:, cols], preferred_element_type=F32).reshape(pf.shape[1:])
            y1s[i] = pf[i, c2].astype(BF16)
            send(y1s.at[i, 0:2], y1r.at[i, 0], i, 0, to_cp)
            send(y1s.at[i, 2:4], y1r.at[i, 1], i, 0, to_cm)

        def sum_col(i):
            got(y1r.at[i], i, 0)
            y2s[i, 0, 0:2] = (pf[i, cp, 0:2] + y1r[i, 0].astype(F32)).astype(BF16)
            y2s[i, 0, 2:4] = pf[i, cp, 2:4].astype(BF16)
            y2s[i, 1, 0:2] = pf[i, cm, 0:2].astype(BF16)
            y2s[i, 1, 2:4] = (pf[i, cm, 2:4] + y1r[i, 1].astype(F32)).astype(BF16)
            send(y2s.at[i, 0], y2r.at[i, 0], i, 1, to_cp)
            send(y2s.at[i, 1], y2r.at[i, 1], i, 1, to_cm)

        def sum_seq(i):
            got(y2r.at[i], i, 1)
            pf[i, c] = pf[i, c] + y2r[i, 0].astype(F32) + y2r[i, 1].astype(F32)
            zs[i] = pf[i, c].astype(BF16)
            for d in range(3):
                send(zs.at[i, (s + d + 1) % 4], zr.at[i, d], i, 2, to_seq[d])

        def share_seq(i):
            got(zr.at[i], i, 2)
            total = pf[i, c, s]
            for d in range(3):
                total = total + zr[i, d].astype(F32)
            gp[i, c, s] = total.astype(BF16)
            for d in range(3):
                send(gp.at[i, c, s], gp.at[i, c, s], i, 3, to_seq[d])

        def share_col(i):
            got(zr.at[i], i, 3)
            send(gp.at[i, c], gp.at[i, c], i, 4, to_cp)
            send(gp.at[i, c], gp.at[i, c], i, 4, to_cm)

        def pass_col(i):
            got(y2r.at[i], i, 4)
            send(gp.at[i, cm, 0:2], gp.at[i, cm, 0:2], i, 5, to_cp)
            send(gp.at[i, cp, 2:4], gp.at[i, cp, 2:4], i, 5, to_cm)

        def complete(i):
            got(y1r.at[i], i, 5)

        def sent():
            for n, copied in enumerate((y1s, y2s, zr, zr, y2r, y1r)):
                remote(copied, copied, c_s.at[n], c_r.at[0, n], to_core).wait_send()

        return (multiply, sum_col, sum_seq, share_seq, share_col, pass_col), complete, sent

    (multiply0, sum_col0, sum_seq0, share_seq0, share_col0, pass_col0), complete0, sent0 = part(
        0, SEQ, pf0, y1s0, y1r0, y2s0, y2r0, zs0, zr0, gp0, c_s0, c_r0
    )
    (multiply1, sum_col1, sum_seq1, share_seq1, share_col1, pass_col1), complete1, sent1 = part(
        SEQ, LIVE, pf1, y1s1, y1r1, y2s1, y2r1, zs1, zr1, gp1, c_s1, c_r1
    )

    def out_copy(i):
        rows = pl.ds(i * COLS if isinstance(i, int) else pl.multiple_of(i * COLS, COLS), COLS)
        return pltpu.make_async_copy(res.at[i], out_ref.at[rows], out_sem.at[0])

    def square(i):
        complete0(i)
        complete1(i)
        gt[:, 0:SEQ] = gp0[i].reshape(SEQ, COLS).T
        gt[:, SEQ:LIVE] = gp1[i].reshape(LIVE - SEQ, COLS).T
        total = None
        for q in range(4):
            one = jnp.dot(gt[...], am[q], preferred_element_type=F32)
            total = one * one if total is None else total + one * one
        res[i] = total * (1.0 / (4 * SEQ))
        out_copy(i).start()

    def masks():
        got_p(ap.at[1 - core], 7)
        shift = jnp.where(half == 0, 0, LIVE - n_first)
        for b in range(3):
            place = lax.broadcasted_iota(jnp.int32, (SEQ, LIVE), 0) + b * SEQ
            source = lax.broadcasted_iota(jnp.int32, (SEQ, LIVE), 1) + shift
            turn = jnp.logical_or(place == source, place == source - LIVE)
            turn = jnp.where(turn, 1.0, 0.0).astype(BF16)
            turned = jnp.dot(turn, ap[...].reshape(LIVE, ap.shape[-1]), preferred_element_type=F32)
            rows = lax.broadcasted_iota(jnp.int32, turned.shape, 0) + b * SEQ
            for q in range(4):
                inside = jnp.logical_or(
                    jnp.logical_and(rows >= own[q][0], rows < own[q][0] + own[q][1]),
                    jnp.logical_and(rows >= rest[q][0], rows < rest[q][0] + rest[q][1]),
                )
                am[q, b * SEQ : (b + 1) * SEQ, :] = jnp.where(inside, turned, 0.0).astype(BF16)

    def p1():
        got_p(kr, 0)
        pa[core] = pa[core] + kr[...]
        send_p(pa.at[core, x2, 0], x1r.at[0], 1, to_xp)
        send_p(pa.at[core, x2, 1], x1r.at[1], 1, to_xm)

    def p2():
        got_p(x1r, 1)
        pa[core, xp, 0] = pa[core, xp, 0] + x1r[0]
        pa[core, xm, 1] = pa[core, xm, 1] + x1r[1]
        send_p(pa.at[core, xp], x2r.at[0], 2, to_xp)
        send_p(pa.at[core, xm], x2r.at[1], 2, to_xm)

    def p3():
        got_p(x2r, 2)
        pa[core, x] = pa[core, x] + x2r[0] + x2r[1]
        send_p(pa.at[core, x, 1 - half], hr, 3, to_half)

    def p4():
        got_p(hr, 3)
        ap[core, x, half] = (pa[core, x, half] + hr[...]).astype(BF16)
        send_p(ap.at[core, x, half], ap.at[core, x, half], 4, to_half)

    def p5():
        got_p(ap.at[core, x, 1 - half], 4)
        send_p(ap.at[core, x], ap.at[core, x], 5, to_xp)
        send_p(ap.at[core, x], ap.at[core, x], 5, to_xm)

    def p6():
        got_p(ap.at[0, 0:2], 5)
        send_p(ap.at[core, xm, 0], ap.at[core, xm, 0], 6, to_xp)
        send_p(ap.at[core, xp, 1], ap.at[core, xp, 1], 6, to_xm)

    def p7():
        got_p(ap.at[0, 0], 6)
        send_p(ap.at[core], ap.at[core], 7, to_core)

    def each(action, low, high):
        if high - low == 1:
            action(low)
        else:

            def one(i, carry):
                action(i)
                return carry

            lax.fori_loop(low, high, one, 0)

    load_ob.start()
    load_ib.start()
    begin()
    begin_rest()
    relay_low(0)
    relay_high(0)
    near_to_core(0)
    far_to_core(0)
    third(0)
    acts_seq()
    other_low()
    from_core(0)
    pack(0)
    load_ob.wait()
    each(multiply0, 0, 4)
    other_high()
    each(multiply0, 4, 7)
    each(sum_col0, 0, 3)
    relay_low(1)
    each(sum_col0, 3, 7)
    relay_high(1)
    each(sum_seq0, 0, 2)
    near_to_core(1)
    far_to_core(1)
    acts_col()
    each(sum_seq0, 2, 4)
    third(1)
    each(sum_seq0, 4, 6)
    from_core(1)
    pack(1)
    each(sum_seq0, 6, 7)
    acts_pass()
    each(share_seq0, 0, 3)
    pack(2)
    each(multiply1, 0, 3)
    each(share_seq0, 3, 7)
    each(multiply1, 3, 7)
    each(sum_col1, 0, 2)
    project_inputs()
    each(sum_col1, 2, 4)
    each(share_col0, 0, 2)
    each(sum_col1, 4, 7)
    each(sum_seq1, 0, 1)
    p1()
    each(share_col0, 2, 4)
    each(sum_seq1, 1, 2)
    each(pass_col0, 0, 1)
    p2()
    each(share_col0, 4, 7)
    each(share_seq1, 0, 1)
    each(sum_seq1, 2, 3)
    each(pass_col0, 1, 3)
    each(sum_seq1, 3, 4)
    each(share_seq1, 1, 2)
    p3()
    each(sum_seq1, 4, 5)
    each(share_seq1, 2, 3)
    each(share_col1, 0, 1)
    each(pass_col0, 3, 5)
    each(sum_seq1, 5, 6)
    each(share_seq1, 3, 4)
    each(share_col1, 1, 2)
    p4()
    each(sum_seq1, 6, 7)
    each(share_seq1, 4, 5)
    each(share_col1, 2, 3)
    each(pass_col0, 5, 7)
    each(share_seq1, 5, 6)
    each(share_col1, 3, 4)
    each(pass_col1, 0, 1)
    p5()
    each(share_seq1, 6, 7)
    each(share_col1, 4, 5)
    each(pass_col1, 1, 2)
    each(share_col1, 5, 6)
    each(pass_col1, 2, 3)
    p6()
    each(share_col1, 6, 7)
    each(pass_col1, 3, 4)
    p7()
    each(pass_col1, 4, 5)
    masks()
    each(square, 0, 1)
    each(pass_col1, 5, 6)
    each(square, 1, 3)
    each(pass_col1, 6, 7)
    each(square, 3, 7)

    for i, copied in ((1, gc.at[0 : 12 * grads_ref.shape[1]]), (2, gc.at[0 : 16 * grads_ref.shape[1]])):
        remote(copied, copied, g_s.at[i], g_r.at[i], to_core).wait_send()
    for i, copied in enumerate((xa.at[c, 0:3], xa.at[0:2], xa.at[0])):
        remote(copied, copied, a_s.at[i], a_r.at[i], to_core).wait_send()
    for i, copied in enumerate((kr, x1r, x2r, hr, ap.at[0, 0, 0], ap.at[0, 0:2], ap.at[0, 0], ap.at[0])):
        remote(copied, copied, p_s.at[i], p_r.at[i], to_core).wait_send()
    sent0()
    sent1()
    pltpu.make_async_copy(res, res, out_sem.at[0]).wait()


def body(grads, acts, out_basis, in_basis, lengths):
    n_seq, n_col = lax.axis_size("seq"), lax.axis_size("col")
    tokens, width = grads.shape
    a_width = acts.shape[1]
    directions, a_directions = out_basis.shape[1], in_basis.shape[1]
    chunks = directions // COLS
    dma = pltpu.SemaphoreType.DMA

    def part(rows):
        piece = (rows // 16, COLS)
        return [
            pltpu.VMEM((chunks, 4, 4, *piece), F32),
            pltpu.VMEM((chunks, 4, *piece), BF16),
            pltpu.VMEM((chunks, 2, 2, *piece), BF16),
            pltpu.VMEM((chunks, 2, 4, *piece), BF16),
            pltpu.VMEM((chunks, 2, 4, *piece), BF16),
            pltpu.VMEM((chunks, 4, *piece), BF16),
            pltpu.VMEM((chunks, 3, *piece), BF16),
            pltpu.VMEM((chunks, 4, 4, *piece), BF16),
        ]

    hbm = pl.BlockSpec(memory_space=pltpu.HBM)
    return pl.pallas_call(
        functools.partial(kernel, chunks),
        out_shape=jax.ShapeDtypeStruct((directions, a_directions), F32),
        in_specs=[pl.BlockSpec(memory_space=pltpu.SMEM), hbm, hbm, hbm, hbm],
        out_specs=hbm,
        scratch_shapes=[
            pltpu.VMEM((4, 2, 2, 2, tokens // 2, width), BF16),
            pltpu.VMEM((n_col, n_seq, tokens, a_width), BF16),
            pltpu.VMEM(out_basis.shape, BF16),
            pltpu.VMEM(in_basis.shape, BF16),
            pltpu.VMEM((LIVE, width), BF16),
            pltpu.VMEM((LIVE, a_width), BF16),
            *part(SEQ),
            *part(LIVE - SEQ),
            pltpu.VMEM((2, 4, 2, PIECE, a_directions), F32),
            pltpu.VMEM((4, 2, PIECE, a_directions), F32),
            pltpu.VMEM((2, PIECE, a_directions), F32),
            pltpu.VMEM((2, 2, PIECE, a_directions), F32),
            pltpu.VMEM((PIECE, a_directions), F32),
            pltpu.VMEM((2, 4, 2, PIECE, a_directions), BF16),
            pltpu.VMEM((4, LIVE, a_directions), BF16),
            pltpu.VMEM((COLS, LIVE), BF16),
            pltpu.VMEM((chunks, COLS, a_directions), F32),
            dma((4,)),
            dma((1,)),
            dma((3,)),
            dma((16,)),
            dma((3,)),
            dma((3,)),
            dma((8,)),
            dma((8,)),
            dma((6,)),
            dma((chunks, 6)),
            dma((6,)),
            dma((chunks, 6)),
        ],
        compiler_params=pltpu.CompilerParams(
            collective_id=0, has_side_effects=True, vmem_limit_bytes=61730 * 1024
        ),
        name="eigen",
    )(lengths, grads.reshape(2, tokens // 2, width), acts, out_basis, in_basis)


def solution(mesh):
    in_specs = (
        P("row", ("seq", "col")),
        P(("seq", "col"), "row"),
        P(("seq", "col"), "row"),
        P("row", ("seq", "col")),
        P(),
    )
    out_specs = P("row", ("seq", "col"))
    return jax.shard_map(body, mesh=mesh, in_specs=in_specs, out_specs=out_specs, check_vma=False)
```

time: 341 us -> 105 us (0.31)
  blocking collectives: 207 us -> 0 us
  Pallas kernels: 0 us -> 100 us
  waiting for transfers between devices: 67.9 us -> 0 us
  matrix products: 32.7 us -> 0 us
  between operations: 13.5 us -> 0.01 us
  starting transfers between devices: 11 us -> 0 us
  other arithmetic: 5.29 us -> 0 us
    psum x1 -> x0, blocking collectives: 168 us -> none  [body(): grad_proj = lax.psum(partial_value, ('seq', 'col')).astype(jnp.bfloat16)]
    pallas_call x0 -> x1, Pallas kernels: none -> 100 us  [body(): pl.pallas_call(functools.partial(kernel, chunks), out_shape=jax.ShapeDtyp...]
    all_to_all x1 -> x0, waiting for transfers between devices: 67.2 us -> none  [sum_at_owner(): lax.all_to_all(tiles, axis, split_axis=0, concat_axis=0, tiled=True)]
    all_to_all x1 -> x0, blocking collectives: 38.8 us -> none  [copy_for_each(): return lax.all_to_all(copies, axis, split_axis=0, concat_axis=0, tiled=True)]
    dot_general x6 -> x0, matrix products: 32.7 us -> none  [the longest x4 18.5 us: accumulate(): lax.dot_general(pair[0], pair[1], (((0,), (0,)), ((), ())), preferred_ele...]
    all_to_all x1 -> x0, starting transfers between devices: 10.9 us -> none  [sum_at_owner(): lax.all_to_all(tiles, axis, split_axis=0, concat_axis=0, tiled=True)]
    div x1 -> x0, other arithmetic: 4.31 us -> none  [body(): return total / (seq_count * SEQ_LEN)]
    unnamed x4 -> x1, local copies, waits for them, and re-layouts: 0.01 us -> 4.25 us
  transfers between devices with their start and end apart: 3 -> 0, of which waited for: 1 -> 0; matrix products, arithmetic and copies ran while one was open for 5% -> 0% of each run, Pallas kernels for 0% -> 0%
where the time goes in v2:
time: 105 us
  Pallas kernels  100 us (95%)
  local copies, waits for them, and re-layouts  4.25 us (4%)
    pallas_call x1, Pallas kernels, body(): pl.pallas_call(functools.partial(kernel, chunks), out_shape=jax.ShapeDtyp...  100 us
    unnamed x1, local copies, waits for them, and re-layouts  4.25 us

profile of v2, /device:TPU:1, one launch (start us, length us, event | category | flops | bytes accessed | tf_op | source)
XLA Modules:
  0.0 104.7 jit_solution(6475502683184716047)
XLA Ops:
  0.0 100.5 %eigen.1 = f32[1792,512]{1,0:T(8,128)} custom-call(s32[4]{0:T(128)} %len_ref.1, bf16[2,32,1792]{2,1,0:T(8,128)(2,1)} %bitcast.1, bf16[64,512]{1,0:T(8,128)(2,1)} %acts_ref.1, bf16[1792,1792]{1,0:T(8,128)(2,1)} %ob_ref.1, bf16[512,512]{1,0:T(8,128)(2,1)} %ib_ref.1), custom_call_target="tpu_custom_call" | custom-call | tf_op jit(solution)/shard_map/eigen/pallas_call | solution.py:479
  100.5 4.2 %copy.7 = f32[1792,512]{1,0:T(8,128)} copy(f32[1792,512]{1,0:T(8,128)} %eigen.1) | data formatting | bytes 7340032

commit v3 on v2

--- a/solution.py
+++ b/solution.py
@@ -37,6 +37,8 @@
     to_half = {"row": row_of(x, 1 - half, core)}
     to_xp, to_xm = {"row": row_of(xp, half, core)}, {"row": row_of(xm, half, core)}
     to_cp, to_cm = {"col": cp}, {"col": cm}
+    even, high_bit = s % 2, s // 2
+    to_near, to_far = {"seq": s + 1 - 2 * even}, {"seq": (s + 2) % 4}
     to_seq = [{"seq": (s + d) % 4} for d in (1, 2, 3)]
 
     def remote(src, dst, send, recv, to):
@@ -200,14 +202,17 @@
                     one = jnp.dot(pick(places, b * SEQ), rows, preferred_element_type=F32)
                     packed = one if packed is None else packed + one
             ac[b * SEQ : (b + 1) * SEQ, :] = packed.astype(BF16)
-        pa[...] = jnp.dot(ac[...], ib[...], preferred_element_type=F32).reshape(pa.shape)
-        send_p(pa.at[1 - core], kr, 0, to_core)
-
-    def send_p(src, dst, i, to):
-        remote(src, dst, p_s.at[i], p_r.at[i], to).start()
-
-    def got_p(dst, i):
-        remote(dst, dst, p_s.at[i], p_r.at[i], to_core).wait_recv()
+        wide = pa.shape[-1]
+        for h in range(2):
+            cols = slice(h * wide, (h + 1) * wide)
+            pa[h] = jnp.dot(ac[...], ib[:, cols], preferred_element_type=F32).reshape(pa.shape[1:])
+            send_p(pa.at[h, 1 - core], kr.at[h], h, 0, to_core)
+
+    def send_p(src, dst, h, i, to):
+        remote(src, dst, p_s.at[i], p_r.at[h, i], to).start()
+
+    def got_p(dst, h, i):
+        remote(dst, dst, p_s.at[i], p_r.at[h, i], to_core).wait_recv()
 
     def part(low, high, pf, y1s, y1r, y2s, y2r, zs, zr, gp, c_s, c_r):
         def send(src, dst, i, n, to):
@@ -235,16 +240,19 @@
         def sum_seq(i):
             got(y2r.at[i], i, 1)
             pf[i, c] = pf[i, c] + y2r[i, 0].astype(F32) + y2r[i, 1].astype(F32)
-            zs[i] = pf[i, c].astype(BF16)
-            for d in range(3):
-                send(zs.at[i, (s + d + 1) % 4], zr.at[i, d], i, 2, to_seq[d])
+            for h in range(2):
+                zs[i, h] = pf[i, c, 1 - even + 2 * h].astype(BF16)
+            send(zs.at[i, 0:2], zr.at[i, 0:2], i, 2, to_near)
+
+        def pass_seq(i):
+            got(zr.at[i, 0:2], i, 2)
+            zs[i, 2] = (pf[i, c, even + 2 * (1 - high_bit)] + zr[i, 1 - high_bit].astype(F32)).astype(BF16)
+            send(zs.at[i, 2], zr.at[i, 2], i, 6, to_far)
+            pf[i, c, s] = pf[i, c, s] + zr[i, high_bit].astype(F32)
 
         def share_seq(i):
-            got(zr.at[i], i, 2)
-            total = pf[i, c, s]
-            for d in range(3):
-                total = total + zr[i, d].astype(F32)
-            gp[i, c, s] = total.astype(BF16)
+            got(zr.at[i, 2], i, 6)
+            gp[i, c, s] = (pf[i, c, s] + zr[i, 2].astype(F32)).astype(BF16)
             for d in range(3):
                 send(gp.at[i, c, s], gp.at[i, c, s], i, 3, to_seq[d])
 
@@ -262,15 +270,15 @@
             got(y1r.at[i], i, 5)
 
         def sent():
-            for n, copied in enumerate((y1s, y2s, zr, zr, y2r, y1r)):
+            for n, copied in enumerate((y1s, y2s, zs.at[:, 0:2], zr, y2r, y1r, zs.at[:, 2])):
                 remote(copied, copied, c_s.at[n], c_r.at[0, n], to_core).wait_send()
 
-        return (multiply, sum_col, sum_seq, share_seq, share_col, pass_col), complete, sent
-
-    (multiply0, sum_col0, sum_seq0, share_seq0, share_col0, pass_col0), complete0, sent0 = part(
+        return (multiply, sum_col, sum_seq, pass_seq, share_seq, share_col, pass_col), complete, sent
+
+    (multiply0, sum_col0, sum_seq0, pass_seq0, share_seq0, share_col0, pass_col0), complete0, sent0 = part(
         0, SEQ, pf0, y1s0, y1r0, y2s0, y2r0, zs0, zr0, gp0, c_s0, c_r0
     )
-    (multiply1, sum_col1, sum_seq1, share_seq1, share_col1, pass_col1), complete1, sent1 = part(
+    (multiply1, sum_col1, sum_seq1, pass_seq1, share_seq1, share_col1, pass_col1), complete1, sent1 = part(
         SEQ, LIVE, pf1, y1s1, y1r1, y2s1, y2r1, zs1, zr1, gp1, c_s1, c_r1
     )
 
@@ -290,59 +298,60 @@
         res[i] = total * (1.0 / (4 * SEQ))
         out_copy(i).start()
 
-    def masks():
-        got_p(ap.at[1 - core], 7)
+    def masks(h):
+        got_p(ap.at[h, 1 - core], h, 7)
+        wide = ap.shape[-1]
         shift = jnp.where(half == 0, 0, LIVE - n_first)
         for b in range(3):
             place = lax.broadcasted_iota(jnp.int32, (SEQ, LIVE), 0) + b * SEQ
             source = lax.broadcasted_iota(jnp.int32, (SEQ, LIVE), 1) + shift
             turn = jnp.logical_or(place == source, place == source - LIVE)
             turn = jnp.where(turn, 1.0, 0.0).astype(BF16)
-            turned = jnp.dot(turn, ap[...].reshape(LIVE, ap.shape[-1]), preferred_element_type=F32)
+            turned = jnp.dot(turn, ap[h].reshape(LIVE, wide), preferred_element_type=F32)
             rows = lax.broadcasted_iota(jnp.int32, turned.shape, 0) + b * SEQ
             for q in range(4):
                 inside = jnp.logical_or(
                     jnp.logical_and(rows >= own[q][0], rows < own[q][0] + own[q][1]),
                     jnp.logical_and(rows >= rest[q][0], rows < rest[q][0] + rest[q][1]),
                 )
-                am[q, b * SEQ : (b + 1) * SEQ, :] = jnp.where(inside, turned, 0.0).astype(BF16)
-
-    def p1():
-        got_p(kr, 0)
-        pa[core] = pa[core] + kr[...]
-        send_p(pa.at[core, x2, 0], x1r.at[0], 1, to_xp)
-        send_p(pa.at[core, x2, 1], x1r.at[1], 1, to_xm)
-
-    def p2():
-        got_p(x1r, 1)
-        pa[core, xp, 0] = pa[core, xp, 0] + x1r[0]
-        pa[core, xm, 1] = pa[core, xm, 1] + x1r[1]
-        send_p(pa.at[core, xp], x2r.at[0], 2, to_xp)
-        send_p(pa.at[core, xm], x2r.at[1], 2, to_xm)
-
-    def p3():
-        got_p(x2r, 2)
-        pa[core, x] = pa[core, x] + x2r[0] + x2r[1]
-        send_p(pa.at[core, x, 1 - half], hr, 3, to_half)
-
-    def p4():
-        got_p(hr, 3)
-        ap[core, x, half] = (pa[core, x, half] + hr[...]).astype(BF16)
-        send_p(ap.at[core, x, half], ap.at[core, x, half], 4, to_half)
-
-    def p5():
-        got_p(ap.at[core, x, 1 - half], 4)
-        send_p(ap.at[core, x], ap.at[core, x], 5, to_xp)
-        send_p(ap.at[core, x], ap.at[core, x], 5, to_xm)
-
-    def p6():
-        got_p(ap.at[0, 0:2], 5)
-        send_p(ap.at[core, xm, 0], ap.at[core, xm, 0], 6, to_xp)
-        send_p(ap.at[core, xp, 1], ap.at[core, xp, 1], 6, to_xm)
-
-    def p7():
-        got_p(ap.at[0, 0], 6)
-        send_p(ap.at[core], ap.at[core], 7, to_core)
+                am[q, b * SEQ : (b + 1) * SEQ, h * wide : (h + 1) * wide] = jnp.where(inside, turned, 0.0).astype(BF16)
+
+    def p1(h):
+        got_p(kr.at[h], h, 0)
+        pa[h, core] = pa[h, core] + kr[h]
+        send_p(pa.at[h, core, x2, 0], x1r.at[h, 0], h, 1, to_xp)
+        send_p(pa.at[h, core, x2, 1], x1r.at[h, 1], h, 1, to_xm)
+
+    def p2(h):
+        got_p(x1r.at[h], h, 1)
+        pa[h, core, xp, 0] = pa[h, core, xp, 0] + x1r[h, 0]
+        pa[h, core, xm, 1] = pa[h, core, xm, 1] + x1r[h, 1]
+        send_p(pa.at[h, core, xp], x2r.at[h, 0], h, 2, to_xp)
+        send_p(pa.at[h, core, xm], x2r.at[h, 1], h, 2, to_xm)
+
+    def p3(h):
+        got_p(x2r.at[h], h, 2)
+        pa[h, core, x] = pa[h, core, x] + x2r[h, 0] + x2r[h, 1]
+        send_p(pa.at[h, core, x, 1 - half], hr.at[h], h, 3, to_half)
+
+    def p4(h):
+        got_p(hr.at[h], h, 3)
+        ap[h, core, x, half] = (pa[h, core, x, half] + hr[h]).astype(BF16)
+        send_p(ap.at[h, core, x, half], ap.at[h, core, x, half], h, 4, to_half)
+
+    def p5(h):
+        got_p(ap.at[h, core, x, 1 - half], h, 4)
+        send_p(ap.at[h, core, x], ap.at[h, core, x], h, 5, to_xp)
+        send_p(ap.at[h, core, x], ap.at[h, core, x], h, 5, to_xm)
+
+    def p6(h):
+        got_p(ap.at[h, 0, 0:2], h, 5)
+        send_p(ap.at[h, core, xm, 0], ap.at[h, core, xm, 0], h, 6, to_xp)
+        send_p(ap.at[h, core, xp, 1], ap.at[h, core, xp, 1], h, 6, to_xm)
+
+    def p7(h):
+        got_p(ap.at[h, 0, 0], h, 6)
+        send_p(ap.at[h, core], ap.at[h, core], h, 7, to_core)
 
     def each(action, low, high):
         if high - low == 1:
@@ -377,69 +386,85 @@
     each(sum_col0, 3, 7)
     relay_high(1)
     each(sum_seq0, 0, 2)
+    acts_col()
     near_to_core(1)
     far_to_core(1)
-    acts_col()
     each(sum_seq0, 2, 4)
     third(1)
     each(sum_seq0, 4, 6)
     from_core(1)
     pack(1)
     each(sum_seq0, 6, 7)
+    each(pass_seq0, 0, 5)
+    pack(2)
     acts_pass()
+    each(pass_seq0, 5, 7)
     each(share_seq0, 0, 3)
-    pack(2)
-    each(multiply1, 0, 3)
+    each(multiply1, 0, 5)
     each(share_seq0, 3, 7)
-    each(multiply1, 3, 7)
+    each(multiply1, 5, 7)
     each(sum_col1, 0, 2)
     project_inputs()
-    each(sum_col1, 2, 4)
+    each(sum_col1, 2, 7)
+    p1(0)
+    p1(1)
+    each(sum_seq1, 0, 1)
     each(share_col0, 0, 2)
-    each(sum_col1, 4, 7)
-    each(sum_seq1, 0, 1)
-    p1()
+    each(sum_seq1, 1, 2)
+    p2(0)
+    each(pass_seq1, 0, 1)
+    p2(1)
+    each(sum_seq1, 2, 3)
+    each(pass_seq1, 1, 2)
+    p3(0)
     each(share_col0, 2, 4)
-    each(sum_seq1, 1, 2)
-    each(pass_col0, 0, 1)
-    p2()
+    each(share_seq1, 0, 1)
+    p3(1)
+    each(sum_seq1, 3, 4)
+    each(pass_seq1, 2, 3)
+    each(share_seq1, 1, 2)
     each(share_col0, 4, 7)
-    each(share_seq1, 0, 1)
-    each(sum_seq1, 2, 3)
-    each(pass_col0, 1, 3)
-    each(sum_seq1, 3, 4)
-    each(share_seq1, 1, 2)
-    p3()
     each(sum_seq1, 4, 5)
+    each(sum_seq1, 5, 6)
+    each(pass_col0, 0, 2)
+    each(sum_seq1, 6, 7)
+    p4(0)
+    each(pass_seq1, 3, 4)
     each(share_seq1, 2, 3)
+    p4(1)
+    each(pass_seq1, 4, 5)
+    each(pass_col0, 2, 4)
+    each(pass_seq1, 5, 6)
     each(share_col1, 0, 1)
-    each(pass_col0, 3, 5)
-    each(sum_seq1, 5, 6)
     each(share_seq1, 3, 4)
+    each(pass_seq1, 6, 7)
+    p5(0)
     each(share_col1, 1, 2)
-    p4()
-    each(sum_seq1, 6, 7)
     each(share_seq1, 4, 5)
+    p5(1)
+    each(pass_col0, 4, 7)
+    each(share_seq1, 5, 6)
     each(share_col1, 2, 3)
-    each(pass_col0, 5, 7)
-    each(share_seq1, 5, 6)
+    each(share_seq1, 6, 7)
+    p6(0)
     each(share_col1, 3, 4)
+    p6(1)
     each(pass_col1, 0, 1)
-    p5()
-    each(share_seq1, 6, 7)
     each(share_col1, 4, 5)
+    p7(0)
     each(pass_col1, 1, 2)
+    p7(1)
     each(share_col1, 5, 6)
+    masks(0)
     each(pass_col1, 2, 3)
-    p6()
     each(share_col1, 6, 7)
+    masks(1)
     each(pass_col1, 3, 4)
-    p7()
+    each(square, 0, 1)
     each(pass_col1, 4, 5)
-    masks()
-    each(square, 0, 1)
+    each(square, 1, 2)
     each(pass_col1, 5, 6)
-    each(square, 1, 3)
+    each(square, 2, 3)
     each(pass_col1, 6, 7)
     each(square, 3, 7)
 
@@ -447,8 +472,8 @@
         remote(copied, copied, g_s.at[i], g_r.at[i], to_core).wait_send()
     for i, copied in enumerate((xa.at[c, 0:3], xa.at[0:2], xa.at[0])):
         remote(copied, copied, a_s.at[i], a_r.at[i], to_core).wait_send()
-    for i, copied in enumerate((kr, x1r, x2r, hr, ap.at[0, 0, 0], ap.at[0, 0:2], ap.at[0, 0], ap.at[0])):
-        remote(copied, copied, p_s.at[i], p_r.at[i], to_core).wait_send()
+    for i, copied in enumerate((kr, x1r, x2r, hr, ap.at[:, 0, 0, 0], ap.at[:, 0, 0:2], ap.at[:, 0, 0], ap.at[:, 0])):
+        remote(copied, copied, p_s.at[i], p_r.at[0, i], to_core).wait_send()
     sent0()
     sent1()
     pltpu.make_async_copy(res, res, out_sem.at[0]).wait()
@@ -470,11 +495,12 @@
             pltpu.VMEM((chunks, 2, 2, *piece), BF16),
             pltpu.VMEM((chunks, 2, 4, *piece), BF16),
             pltpu.VMEM((chunks, 2, 4, *piece), BF16),
-            pltpu.VMEM((chunks, 4, *piece), BF16),
+            pltpu.VMEM((chunks, 3, *piece), BF16),
             pltpu.VMEM((chunks, 3, *piece), BF16),
             pltpu.VMEM((chunks, 4, 4, *piece), BF16),
         ]
 
+    a_piece = (PIECE, a_directions // 2)
     hbm = pl.BlockSpec(memory_space=pltpu.HBM)
     return pl.pallas_call(
         functools.partial(kernel, chunks),
@@ -490,12 +516,12 @@
             pltpu.VMEM((LIVE, a_width), BF16),
             *part(SEQ),
             *part(LIVE - SEQ),
-            pltpu.VMEM((2, 4, 2, PIECE, a_directions), F32),
-            pltpu.VMEM((4, 2, PIECE, a_directions), F32),
-            pltpu.VMEM((2, PIECE, a_directions), F32),
-            pltpu.VMEM((2, 2, PIECE, a_directions), F32),
-            pltpu.VMEM((PIECE, a_directions), F32),
-            pltpu.VMEM((2, 4, 2, PIECE, a_directions), BF16),
+            pltpu.VMEM((2, 2, 4, 2, *a_piece), F32),
+            pltpu.VMEM((2, 4, 2, *a_piece), F32),
+            pltpu.VMEM((2, 2, *a_piece), F32),
+            pltpu.VMEM((2, 2, 2, *a_piece), F32),
+            pltpu.VMEM((2, *a_piece), F32),
+            pltpu.VMEM((2, 2, 4, 2, *a_piece), BF16),
             pltpu.VMEM((4, LIVE, a_directions), BF16),
             pltpu.VMEM((COLS, LIVE), BF16),
             pltpu.VMEM((chunks, COLS, a_directions), F32),
@@ -506,11 +532,11 @@
             dma((3,)),
             dma((3,)),
             dma((8,)),
-            dma((8,)),
-            dma((6,)),
-            dma((chunks, 6)),
-            dma((6,)),
-            dma((chunks, 6)),
+            dma((2, 8)),
+            dma((7,)),
+            dma((chunks, 7)),
+            dma((7,)),
+            dma((chunks, 7)),
         ],
         compiler_params=pltpu.CompilerParams(
             collective_id=0, has_side_effects=True, vmem_limit_bytes=61730 * 1024

time: 105 us -> 99.3 us (0.946)
  Pallas kernels: 100 us -> 94.9 us
    pallas_call x1, Pallas kernels: 100 us -> 94.9 us  [body(): pl.pallas_call(functools.partial(kernel, chunks), out_shape=jax.ShapeDtyp...]
where the time goes in v3:
time: 99.3 us; the launch traced here: 99.2 us
  Pallas kernels  94.9 us (96%)
  local copies, waits for them, and re-layouts  4.25 us (4%)
    pallas_call x1, Pallas kernels, body(): pl.pallas_call(functools.partial(kernel, chunks), out_shape=jax.ShapeDtyp...  94.9 us
    unnamed x1, local copies, waits for them, and re-layouts  4.25 us

profile of v3, /device:TPU:1, one launch (start us, length us, event | category | flops | bytes accessed | tf_op | source)
XLA Modules:
  0.0 99.2 jit_solution(6074035781988704037)
XLA Ops:
  0.0 94.9 %eigen.1 = f32[1792,512]{1,0:T(8,128)} custom-call(s32[4]{0:T(128)} %len_ref.1, bf16[2,32,1792]{2,1,0:T(8,128)(2,1)} %bitcast.1, bf16[64,512]{1,0:T(8,128)(2,1)} %acts_ref.1, bf16[1792,1792]{1,0:T(8,128)(2,1)} %ob_ref.1, bf16[512,512]{1,0:T(8,128)(2,1)} %ib_ref.1), custom_call_target="tpu_custom_call" | custom-call | tf_op jit(solution)/shard_map/eigen/pallas_call | solution.py:505
  94.9 4.2 %copy.7 = f32[1792,512]{1,0:T(8,128)} copy(f32[1792,512]{1,0:T(8,128)} %eigen.1) | data formatting | bytes 7340032

commit v4 on v3

--- a/solution.py
+++ b/solution.py
@@ -429,9 +429,9 @@
     each(pass_col0, 0, 2)
     each(sum_seq1, 6, 7)
     p4(0)
+    p4(1)
     each(pass_seq1, 3, 4)
     each(share_seq1, 2, 3)
-    p4(1)
     each(pass_seq1, 4, 5)
     each(pass_col0, 2, 4)
     each(pass_seq1, 5, 6)
@@ -448,16 +448,16 @@
     each(share_seq1, 6, 7)
     p6(0)
     each(share_col1, 3, 4)
+    each(share_col1, 4, 5)
     p6(1)
     each(pass_col1, 0, 1)
-    each(share_col1, 4, 5)
+    each(share_col1, 5, 6)
     p7(0)
     each(pass_col1, 1, 2)
+    each(share_col1, 6, 7)
     p7(1)
-    each(share_col1, 5, 6)
     masks(0)
     each(pass_col1, 2, 3)
-    each(share_col1, 6, 7)
     masks(1)
     each(pass_col1, 3, 4)
     each(square, 0, 1)

time: 99.3 us -> 98.8 us (level)
  no operation moved by 1% of the time
where the time goes in v4:
time: 98.8 us; the launch traced here: 98.6 us
  Pallas kernels  94.4 us (96%)
  local copies, waits for them, and re-layouts  4.25 us (4%)
    pallas_call x1, Pallas kernels, body(): pl.pallas_call(functools.partial(kernel, chunks), out_shape=jax.ShapeDtyp...  94.4 us
    unnamed x1, local copies, waits for them, and re-layouts  4.25 us

profile of v4, /device:TPU:1, one launch (start us, length us, event | category | flops | bytes accessed | tf_op | source)
XLA Modules:
  0.0 98.6 jit_solution(18217906960543573838)
XLA Ops:
  0.0 94.4 %eigen.1 = f32[1792,512]{1,0:T(8,128)} custom-call(s32[4]{0:T(128)} %len_ref.1, bf16[2,32,1792]{2,1,0:T(8,128)(2,1)} %bitcast.1, bf16[64,512]{1,0:T(8,128)(2,1)} %acts_ref.1, bf16[1792,1792]{1,0:T(8,128)(2,1)} %ob_ref.1, bf16[512,512]{1,0:T(8,128)(2,1)} %ib_ref.1), custom_call_target="tpu_custom_call" | custom-call | tf_op jit(solution)/shard_map/eigen/pallas_call | solution.py:505
  94.4 4.2 %copy.7 = f32[1792,512]{1,0:T(8,128)} copy(f32[1792,512]{1,0:T(8,128)} %eigen.1) | data formatting | bytes 7340032
